TPU v7x, 32 devices: a whole 2x2x4 slice. The times are simulated.
32 devices in a mesh: col: 4 (over y, x), row: 8 (over z, core).
Axes of the slice: x: 2, y: 2, z: 4, core: 2. Of those that a mesh axis runs over, the one named last changes fastest.
Arguments:
- covariance: float32 [12288, 12288], P('row', 'col'), may hold values from -2 to 2, as said below
- wfs_map: int32 [12288], P('row'), may hold values from 0 to 5
- noise_var: float32 [6], replicated, may hold values from 0.5 to 2
- targets: float32 [12288, 2048], P('row', 'col'), may hold values from -0.6 to 0.6
- target_pos: float32 [2, 2048], replicated, may hold values from -1 to 1
- layer_strength: float32 [35], replicated, may hold values from 0.005 to 0.05
- layer_scale: float32 [35], replicated, may hold values from 0.2 to 2
- tile_layer: int32 [16], replicated, may hold values from 0 to 34
Outputs:
- updated: float32 [12288, 12288], P('row', 'col')
- panel_factor: float32 [12288, 256], P('row')
- reconstructor: float32 [12288, 2048], P('row', 'col')
- error_cov: float32 [2048, 2048], P('row', 'col')
Inputs may be any that keep to these rules, and one draw needn't show every extreme that they name: `covariance`: symmetric and positive semidefinite; its diagonal lies between 0.5 and 2.
All inputs are finite; a program needn't handle non-finite values.
Results may differ from a plain program's by a relative error of at most 0.0003.
Values sent between devices are 32-bit elements; how exact they have to be, the bound alone decides.
A program may use at most 128 MiB of HBM per device.

v0:
```python
import jax
import jax.numpy as jnp
from jax import lax
from jax.sharding import PartitionSpec as P

PB = 256
TILE = 128


precise = lax.Precision.HIGHEST


def broadcast(shard, axis, root):
    mine = lax.axis_index(axis) == root
    return lax.psum(jnp.where(mine, shard, jnp.zeros_like(shard)), axis)


def lookup(values, indices, entries):
    one_hot = (indices[:, None] == jnp.arange(entries, dtype=jnp.int32)[None, :]).astype(
        jnp.float32
    )
    return jnp.dot(one_hot, values, precision=precise)


def target_covariance(pos_rows, pos_cols, layer_rows, layer_cols, layer_strength, layer_scale):
    distance = (pos_rows[0][:, None] - pos_cols[0][None, :]) ** 2 + (
        pos_rows[1][:, None] - pos_cols[1][None, :]
    ) ** 2
    lowest = jnp.minimum(layer_rows[:, None], layer_cols[None, :])
    levels = jnp.arange(layer_strength.shape[0], dtype=jnp.int32)
    weights = layer_strength[:, None, None] / (
        1.0 + distance[None] / (layer_scale * layer_scale)[:, None, None]
    )
    return jnp.sum(jnp.where(levels[:, None, None] <= lowest[None], weights, 0.0), axis=0)


def local(
    covariance, wfs_map, noise_var, targets, target_pos, layer_strength, layer_scale, tile_layer
):
    row_count, col_count = covariance.shape
    target_width = targets.shape[1]
    row_index = lax.axis_index("row")
    col_index = lax.axis_index("col")
    row_ids = row_index * row_count + jnp.arange(row_count, dtype=jnp.int32)
    col_ids = col_index * col_count + jnp.arange(col_count, dtype=jnp.int32)
    noise_rows = lookup(noise_var, wfs_map, noise_var.shape[0])
    on_diagonal = row_ids[:, None] == col_ids[None, :]
    matrix = covariance + jnp.where(on_diagonal, noise_rows[:, None], 0.0)
    diag_block = broadcast(matrix[:PB, :PB], ("col", "row"), 0)
    factor = jnp.linalg.cholesky(diag_block)
    solved = jax.scipy.linalg.solve_triangular(factor, matrix[:, :PB].T, lower=True).T
    top_rows = jnp.concatenate([factor, jnp.zeros((row_count - PB, PB), jnp.float32)], axis=0)
    own_rows = jnp.where(row_ids[:, None] < PB, top_rows, solved)
    panel_rows = broadcast(own_rows, "col", 0)
    head_rows = jax.scipy.linalg.solve_triangular(factor, targets[:PB], lower=True)
    head_cols = broadcast(head_rows, "row", 0)
    row_ratio = col_count // row_count
    pieces = []
    for within in range(row_ratio):
        pieces.append(broadcast(panel_rows, "row", col_index * row_ratio + within))
    col_panel = jnp.concatenate(pieces, axis=0)
    product = lax.dot_general(
        panel_rows,
        col_panel,
        (((1,), (1,)), ((), ())),
        precision=precise,
        preferred_element_type=jnp.float32,
    )
    fill_cols = jnp.concatenate(
        [panel_rows, jnp.zeros((row_count, col_count - PB), jnp.float32)], axis=1
    )
    trailing = (row_ids[:, None] >= PB) & (col_ids[None, :] >= PB)
    updated = jnp.where(
        trailing, matrix - product, jnp.where(col_ids[None, :] < PB, fill_cols, 0.0)
    )
    head_top = jnp.concatenate(
        [head_cols, jnp.zeros((row_count - PB, target_width), jnp.float32)], axis=0
    )
    reduced = targets - jnp.dot(panel_rows, head_cols, precision=precise)
    reconstructor = jnp.where(row_ids[:, None] < PB, head_top, reduced)
    error_rows = target_width * lax.axis_size("col") // lax.axis_size("row")
    row_start = row_index * error_rows
    gathered = lax.all_gather(head_cols, "col", axis=1, tiled=True)
    head_needed = lax.dynamic_slice_in_dim(gathered, row_start, error_rows, 1)
    layer_all = jnp.repeat(tile_layer, TILE)
    col_start = col_index * target_width
    pos_rows = lax.dynamic_slice_in_dim(target_pos, row_start, error_rows, 1)
    pos_cols = lax.dynamic_slice_in_dim(target_pos, col_start, target_width, 1)
    layer_rows = lax.dynamic_slice_in_dim(layer_all, row_start, error_rows, 0)
    layer_cols = lax.dynamic_slice_in_dim(layer_all, col_start, target_width, 0)
    target_cov = target_covariance(
        pos_rows, pos_cols, layer_rows, layer_cols, layer_strength, layer_scale
    )
    error_cov = target_cov - lax.dot_general(
        head_needed,
        head_cols,
        (((0,), (0,)), ((), ())),
        precision=precise,
        preferred_element_type=jnp.float32,
    )
    return (updated, panel_rows, reconstructor, error_cov)


def solution(mesh):
    placed = (P("row", "col"), P("row"), P(), P("row", "col"), P(), P(), P(), P())
    return jax.shard_map(
        local,
        mesh=mesh,
        in_specs=placed,
        out_specs=(P("row", "col"), P("row", None), P("row", "col"), P("row", "col")),
        check_vma=False,
    )
```

profile of v0, /device:TPU:30, one launch (start us, length us, event | category | flops | bytes accessed | tf_op | source)
XLA Modules:
  0.0 450.4 jit_solution(13799213461275540915)
XLA Ops:
  7.2 0.0 copy-start
  7.2 0.0 all-reduce.9.cloned.1.call-start
  7.3 18.6 %copy.21 = f32[1536,3072]{0,1:T(8,128)} copy(f32[1536,3072]{1,0:T(8,128)} %param.8) | data formatting | bytes 37748736 | tf_op args[0]
  25.9 0.0 copy-done.6
  25.9 0.0 copy-done.7
  25.9 0.6 convolution_reduce_fusion
  26.6 8.3 %select_add_fusion = f32[1536,3072]{0,1:T(8,128)S(1)} fusion(f32[1536,3072]{0,1:T(8,128)} %copy.21, f32[1536]{0:T(1024)S(1)} %convolution_reduce_fusion, s32[1536]{0:T(1024)S(1)} %iota_add_fusion.1, s32[3072]{0:T(1024)S(1)} %iota_add_fusion), kind=kLoop, calls=%fused_computation.3 | loop fusion | flops 14155776 | bytes 37773312 | tf_op jit(solution)/shard_map/add | solution.py:48
  34.8 0.0 copy-start.2
  34.8 6.8 %copy-done.2 = f32[1536,3072]{0,1:T(8,128)} copy-done((f32[1536,3072]{0,1:T(8,128)}, f32[1536,3072]{0,1:T(8,128)S(1)}, u32[]{:S(2)}) %copy-start.2) | copy-done | bytes 18874392
  41.7 0.7 slice_select_fusion
  42.4 0.0 all-reduce.9.cloned.1.call-update
  42.4 0.0 all-reduce.11.cloned.1.call-start
  42.5 1.5 slice_bitcast_fusion
  44.0 124.1 %all-reduce.9.cloned.1.call-done = f32[256,256]{0,1:T(8,128)} async-done(((f32[256,256]{0,1:T(8,128)}), f32[256,256]{0,1:T(8,128)}) %all-reduce.9.cloned.1.call-update) | async-done | bytes 262160 | tf_op jit(solution)/shard_map/psum | solution.py:15
  168.1 1.1 copy.22
  169.2 1.0 fusion.12
  170.2 11.7 %cholesky.49 = f32[128,128]{1,0:T(8,128)S(1)} custom-call(f32[128,128]{1,0:T(8,128)S(1)} %cholesky.115), custom_call_target="Cholesky" | custom-call | tf_op jit(solution)/shard_map/jit(cholesky)/cholesky | solution.py:50
  181.9 0.1 copy.23
  182.0 9.8 %custom-call.18 = f32[1,128,128]{1,2,0:T(8,128)S(1)} custom-call(f32[1,128,128]{2,1,0:T(8,128)S(1)} %get-tuple-element.46), custom_call_target="InvertDiagBlocksLowerTriangular" | custom-call | tf_op jit(solution)/shard_map/jit(cholesky)/cholesky | solution.py:50
  191.9 0.2 fusion.17
  192.1 0.1 copy.24
  192.2 0.3 convolution_subtract_fusion.4
  192.4 11.7 %cholesky.103 = f32[128,128]{1,0:T(8,128)S(1)} custom-call(f32[128,128]{1,0:T(8,128)S(1)} %convolution_subtract_fusion.4), custom_call_target="Cholesky" | custom-call | tf_op jit(solution)/shard_map/jit(cholesky)/cholesky | solution.py:50
  204.2 0.1 copy.25
  204.4 0.6 compare_reduce_fusion
  206.3 0.1 triangular_solve.57
  206.4 4.4 while.1
  206.6 0.6 fusion.43
  207.1 1.4 dynamic-slice.15
  208.5 0.1 copy.33
  208.7 0.6 fusion.43
  209.3 1.4 dynamic-slice.15
  210.6 0.1 copy.33
  210.8 19.7 %custom-call.19 = f32[2,128,128]{1,2,0:T(8,128)S(1)} custom-call(f32[2,128,128]{2,1,0:T(8,128)S(1)} %get-tuple-element.11), custom_call_target="InvertDiagBlocksLowerTriangular" | custom-call | tf_op jit(solution)/shard_map/jit(_solve_triangular)/triangular_solve | solution.py:51
  230.5 0.8 fusion.9
  231.3 0.8 convolution_subtract_fusion.1
  232.2 0.8 fusion.21
  233.0 1.3 fusion.8
  234.3 0.0 all-reduce.11.cloned.1.call-update
  234.4 0.0 all-reduce.13.cloned.1.call-start
  234.4 1.4 fusion.14
  235.8 1.4 convolution_subtract_fusion.3
  237.2 0.4 fusion.20
  237.6 0.8 maximum_select_fusion
  238.5 56.8 %all-reduce.11.cloned.1.call-done = f32[1536,256]{0,1:T(8,128)} async-done(((f32[1536,256]{0,1:T(8,128)}), f32[1536,256]{0,1:T(8,128)}) %all-reduce.11.cloned.1.call-update) | async-done | bytes 1572880 | tf_op jit(solution)/shard_map/psum | solution.py:15
  295.3 3.5 broadcast_select_fusion.1
  298.7 0.0 all-reduce.13.cloned.1.call-update
  298.8 0.0 all-gather.2.cloned.1.call-start
  298.8 0.0 copy-done.8
  298.8 0.1 broadcast_bitcast_fusion
  298.9 0.1 dynamic_slice.16
  299.0 0.1 dynamic_slice.15
  299.1 0.9 constant_dynamic-slice_fusion.1
  300.0 0.8 constant_dynamic-slice_fusion.2
  300.8 0.1 broadcast_minimum_fusion
  300.9 0.2 multiply_add_fusion
  301.1 84.6 %all-reduce.13.cloned.1.call-done = (f32[1536,256]{0,1:T(8,128)}, f32[1536,256]{0,1:T(8,128)}, f32[256,512]{1,0:T(8,128)}) async-done(((f32[1536,256]{0,1:T(8,128)}, f32[1536,256]{0,1:T(8,128)}, f32[256,512]{1,0:T(8,128)}), (f32[1536,256]{0,1:T(8,128)}, f32[1536,256]{0,1:T(8,128)}, f32[256,512]{1,0:T(8,128)})) %all-reduce.13.cloned.1.call-update) | async-done | bytes 3670032 | tf_op jit(solution)/shard_map/psum | solution.py:15
  385.7 0.0 all-gather.2.cloned.1.call-update
  385.7 4.9 %fusion.2 = f32[256,512]{1,0:T(8,128)S(1)} fusion(f32[35]{0:T(128)S(1)} %mul.28, f32[256,512]{1,0:T(8,128)S(1)} %multiply_add_fusion, f32[35]{0:T(128)S(1)} %copy-done.5, s32[256,512]{1,0:T(8,128)S(1)} %broadcast_minimum_fusion), kind=kLoop, calls=%fused_computation.8 | loop fusion | flops 27394048 | bytes 1573144 | tf_op jit(solution)/shard_map/reduce_sum | solution.py:34
  390.7 1.6 copy.29
  392.3 23.9 %select_select_fusion = f32[1536,3072]{0,1:T(8,128)} fusion(f32[1536,256]{0,1:T(8,128)S(1)} %copy-done.3, f32[1536,3072]{0,1:T(8,128)} %copy-done.2, pred[3072]{0:T(1024)(128)(4,1)S(1)} %get-tuple-element.51, pred[1536]{0:T(1024)(128)(4,1)S(1)} %fusion.27, pred[3072]{0:T(1024)(128)(4,1)S(1)} %get-tuple-element.52, f32[1536,256]{0,1:T(8,128)} %get-tuple-element.36, ...), kind=kOutput, calls=%fused_computation.2 | convolution fusion | flops 14515175424 | bytes 42475008 | tf_op jit(solution)/shard_map/dot_general | solution.py:62
  416.2 18.7 %copy.28 = f32[1536,3072]{1,0:T(8,128)} copy(f32[1536,3072]{0,1:T(8,128)} %select_select_fusion) | data formatting | bytes 37748736
  434.9 6.5 %fusion.3 = f32[1536,512]{1,0:T(8,128)} fusion(f32[1536,512]{1,0:T(8,128)} %param.11, f32[1536,256]{0,1:T(8,128)S(1)} %copy-done.3, f32[256,512]{1,0:T(8,128)S(1)} %copy-done.4, pred[1536]{0:T(1024)(128)(4,1)S(1)} %fusion.26), kind=kOutput, calls=%fused_computation.10 | convolution fusion | flops 2417491968 | bytes 8390144 | tf_op jit(solution)/shard_map/dot_general | solution.py:79
  441.5 2.4 convolution_subtract_fusion.2
  (32 shorter events, 0.3 us)
Async XLA Ops:
  7.2 291.7 %copy-start = (s32[16]{0:T(128)S(1)}, s32[16]{0:T(128)}, u32[]{:S(2)}) copy-start(s32[16]{0:T(128)} %param.15) | copy-start | bytes 196
  7.2 160.9 %all-reduce.9.cloned.1.call-start = ((), (), s32[]{:S(2)}) async-start(), calls=%async_computation | async-start | bytes 524288 | tf_op jit(solution)/shard_map/psum | solution.py:15
  7.2 18.7 %copy-start.6 = (s32[1536]{0:T(1024)S(1)}, s32[1536]{0:T(1024)}, u32[]{:S(2)}) copy-start(s32[1536]{0:T(1024)} %param.9) | copy-start | bytes 18436
  7.2 18.7 %copy-start.7 = (f32[6]{0:T(128)S(1)}, f32[6]{0:T(128)}, u32[]{:S(2)}) copy-start(f32[6]{0:T(128)} %param.10) | copy-start | bytes 76
  34.8 6.9 %copy-start.2 = (f32[1536,3072]{0,1:T(8,128)}, f32[1536,3072]{0,1:T(8,128)S(1)}, u32[]{:S(2)}) copy-start(f32[1536,3072]{0,1:T(8,128)S(1)} %select_add_fusion) | copy-start | bytes 56623108
  42.4 252.8 %all-reduce.11.cloned.1.call-start = ((), (), s32[]{:S(2)}) async-start(), calls=%async_computation.1 | async-start | bytes 3145728 | tf_op jit(solution)/shard_map/psum | solution.py:15
  234.4 151.3 %all-reduce.13.cloned.1.call-start = ((), (), s32[]{:S(2)}) async-start(), calls=%async_computation.3 | async-start | bytes 7340032 | tf_op jit(solution)/shard_map/psum | solution.py:15
  238.5 60.4 %copy-start.8 = (f32[35]{0:T(128)S(1)}, f32[35]{0:T(128)}, u32[]{:S(2)}) copy-start(f32[35]{0:T(128)} %param.14) | copy-start | bytes 424
  298.7 87.0 %copy-start.5 = (f32[35]{0:T(128)S(1)}, f32[35]{0:T(128)}, u32[]{:S(2)}) copy-start(f32[35]{0:T(128)} %param.13) | copy-start | bytes 424
  298.7 91.9 %copy-start.3 = (f32[1536,256]{0,1:T(8,128)S(1)}, f32[1536,256]{0,1:T(8,128)}, u32[]{:S(2)}) copy-start(f32[1536,256]{0,1:T(8,128)} %all-reduce.11.cloned.1.call-done) | copy-start | bytes 4718596
  298.8 142.7 %all-gather.2.cloned.1.call-start = ((), (), s32[]{:S(2)}) async-start(), calls=%async_computation.2 | async-start | bytes 2621440 | tf_op jit(solution)/shard_map/all_gather | solution.py:83
  416.2 18.7 %copy-start.4 = (f32[256,512]{1,0:T(8,128)S(1)}, f32[256,512]{1,0:T(8,128)}, u32[]{:S(2)}) copy-start(f32[256,512]{1,0:T(8,128)} %get-tuple-element.38) | copy-start | bytes 1572868
  416.2 27.6 %copy-start.1 = (s32[16]{0:T(128)S(1)}, s32[16]{0:T(128)}, u32[]{:S(2)}) copy-start(s32[16]{0:T(128)} %param.15) | copy-start | bytes 196
Sparse Core Ops, SparseCore 0:
  42.5 125.5 all-reduce.8
  234.5 60.7 all-reduce.10
  298.9 86.7 all-reduce.12
  387.4 35.1 all-gather.1
where the time goes:
time: 454 us; the launch traced here: 450 us
  waiting for transfers between devices  266 us (59%)
  other arithmetic  74.5 us (16%)
  local copies, waits for them, and re-layouts  55 us (12%)
  matrix products  39.6 us (9%)
  between operations  15.4 us (3%)
    psum x3, waiting for transfers between devices, broadcast(): return lax.psum(jnp.where(mine, shard, jnp.zeros_like(shard)), axis)  265 us
    unnamed x21, local copies, waits for them, and re-layouts  45.8 us
    another operation x6, other arithmetic, local(): factor = jnp.linalg.cholesky(diag_block)  33.9 us
    dot_general x1, matrix products, local(): lax.dot_general(panel_rows, col_panel, (((1,), (1,)), ((), ())), precisio...  23.9 us
    another operation x3, other arithmetic, local(): jax.scipy.linalg.solve_triangular(factor, matrix[:, :PB].T, lower=True)  19.7 us
  transfers between devices with their start and end apart: 4, of which 3 were waited for; matrix products, arithmetic and copies ran while one was open for 14% of the time, Pallas kernels for 0%

commit v1 on v0

v1 whole, which is shorter than its diff:
```python
import functools

import jax
import jax.numpy as jnp
from jax import lax
from jax.experimental import pallas as pl
from jax.experimental.pallas import tpu as pltpu
from jax.sharding import PartitionSpec as P

PB = 256
TILE = 128
HALF = PB // 2
ROWS = 128
CHUNKS = 8
ROW_CHUNKS = 6
SEGMENT = 16

MESH = pl.DeviceIdType.MESH
precise = lax.Precision.HIGHEST


def dot(a, b, dims=((1,), (0,))):
    return lax.dot_general(
        a, b, (dims, ((), ())), precision=precise, preferred_element_type=jnp.float32
    )


def chunks_of(count):
    return max(n for n in range(1, CHUNKS + 1) if count // 128 % n == 0)


def split(x):
    high = x.astype(jnp.bfloat16)
    return high, (x - high.astype(jnp.float32)).astype(jnp.bfloat16)


def dot_split(a, b):
    total = jnp.dot(a[0], b[0], preferred_element_type=jnp.float32)
    total += jnp.dot(a[1], b[0], preferred_element_type=jnp.float32)
    return total + jnp.dot(a[0], b[1], preferred_element_type=jnp.float32)


def target_covariance(pos_rows, pos_cols, layer_rows, layer_cols, layer_strength, layer_scale):
    distance = (pos_rows[0][:, None] - pos_cols[0][None, :]) ** 2 + (
        pos_rows[1][:, None] - pos_cols[1][None, :]
    ) ** 2
    lowest = jnp.minimum(layer_rows[:, None], layer_cols[None, :])
    levels = jnp.arange(layer_strength.shape[0], dtype=jnp.int32)
    weights = layer_strength[:, None, None] / (
        1.0 + distance[None] / (layer_scale * layer_scale)[:, None, None]
    )
    return jnp.sum(jnp.where(levels[:, None, None] <= lowest[None], weights, 0.0), axis=0)


def gray_neighbours(c, n):
    position = c * 0
    after = c * 0
    before = c * 0
    ring = [i ^ (i >> 1) for i in range(n)]
    for i, node in enumerate(ring):
        position = jnp.where(c == node, i, position)
        after = jnp.where(c == node, ring[(i + 1) % n], after)
        before = jnp.where(c == node, ring[(i - 1) % n], before)
    return position, after, before


def pivots(s_ref, m_ref, r_ref, start, count):
    n = s_ref.shape[0]
    lanes = lax.broadcasted_iota(jnp.int32, (n, n), 1)
    lane = lax.broadcasted_iota(jnp.int32, (1, n), 1)
    down = lax.broadcasted_iota(jnp.int32, (n, 1), 0)

    def step(k, carry):
        row = s_ref[pl.ds(k, 1), :]
        inverse_row = m_ref[pl.ds(k, 1), :]
        whole = s_ref[...]
        column = jnp.sum(jnp.where(lanes == k, whole, 0.0), axis=1, keepdims=True)
        pivot = jnp.sum(jnp.where(lane == k, row, 0.0), axis=1, keepdims=True)
        root = lax.rsqrt(pivot)
        factor = jnp.where(down > k, column * (1.0 / pivot), 0.0)
        r_ref[pl.ds(k, 1), :] = jnp.where(lane >= k, row * root, 0.0)
        s_ref[...] = whole - factor * row
        scaled = m_ref[...] - factor * inverse_row
        m_ref[...] = jnp.where(down == k, scaled * root, scaled)
        return carry

    lax.fori_loop(start, start + count, step, 0)


def exchange_kernel(
    n_row,
    n_col,
    cov,
    targets,
    diag,
    row_raw,
    col_raw,
    head_raw,
    need_raw,
    factor_ref,
    inverse_ref,
    blocks,
    s_ref,
    m_ref,
    r_ref,
    local_sem,
    diag_send,
    diag_recv,
    col_send,
    col_recv,
    row_send,
    row_recv,
    need_send,
    need_recv,
):
    r = lax.axis_index("row")
    c = lax.axis_index("col")
    row_count = row_raw.shape[0]
    col_count = col_raw.shape[1]
    width = head_raw.shape[1]
    need = need_raw.shape[1]
    col_chunks = chunks_of(col_count)
    even = lax.rem(r, 2) == 0
    place, after, before = gray_neighbours(c, n_col)
    far_row = jnp.minimum(r + 2, n_row - 1)
    near_row = jnp.where(even, r + 1, r - 1)

    head_copy = pltpu.make_async_copy(targets.at[pl.ds(0, PB), :], head_raw, local_sem.at[0])
    col_copy = pltpu.make_async_copy(cov.at[pl.ds(0, PB), :], col_raw, local_sem.at[1])
    row_copy = pltpu.make_async_copy(cov.at[:, pl.ds(0, PB)], row_raw, local_sem.at[2])
    pl.when(r == 0)(lambda: (head_copy.start(), col_copy.start(), None)[-1])
    pl.when(c == 0)(lambda: (row_copy.start(), None)[-1])

    barrier = pltpu.get_barrier_semaphore()
    for k in range(1, n_row):
        pl.semaphore_signal(
            barrier, inc=1, device_id=(c, lax.rem(r + k, n_row)), device_id_type=MESH
        )
    for k in range(1, n_col):
        pl.semaphore_signal(
            barrier, inc=1, device_id=(lax.rem(c + k, n_col), r), device_id_type=MESH
        )
    pl.semaphore_wait(barrier, n_row + n_col - 2)

    def remote(src, dst, send, recv, col, row):
        return pltpu.make_async_remote_copy(
            src_ref=src,
            dst_ref=dst,
            send_sem=send,
            recv_sem=recv,
            device_id=(col, row),
            device_id_type=MESH,
        )

    def chain(src, dst, send, recv):
        return (
            remote(src, dst, send.at[0], recv, c, far_row),
            remote(src, dst, send.at[1], recv, c, near_row),
        )

    def chain_start(copies, allowed):
        pl.when(allowed & even & (r + 2 < n_row))(lambda: (copies[0].start(), None)[-1])
        pl.when(allowed & even & (r + 1 < n_row))(lambda: (copies[1].start(), None)[-1])

    def chain_end(copies, allowed):
        pl.when(allowed & even & (r + 2 < n_row))(lambda: (copies[0].wait_send(), None)[-1])
        pl.when(allowed & even & (r + 1 < n_row))(lambda: (copies[1].wait_send(), None)[-1])

    quarters = [(0, 0), (HALF, 0), (HALF, HALF)]

    def diag_chain(i, source):
        dst = blocks.at[i]
        src = dst
        if source:
            src = diag.at[pl.ds(quarters[i][0], HALF), pl.ds(quarters[i][1], HALF)]
        return src, dst

    def diag_copies(i, source):
        src, dst = diag_chain(i, source)
        down = chain(src, dst, diag_send.at[i], diag_recv.at[i])
        across = [
            remote(src, dst, diag_send.at[i, 1 + k], diag_recv.at[i], k, r)
            for k in range(1, n_col)
        ]
        return down, across

    def diag_start(i, source, allowed):
        down, across = diag_copies(i, source)
        chain_start(down, allowed)
        for copy in across:
            pl.when(allowed)(lambda copy=copy: (copy.start(), None)[-1])

    def diag_wait(i):
        @pl.when((r > 0) | (c > 0))
        def _():
            diag_copies(i, False)[0][0].wait_recv()

    first = (r == 0) & (c == 0)
    for i in range(3):
        diag_start(i, True, first)

    chunk = col_count // col_chunks

    def col_copies(j, source):
        if j == 0:
            src = targets.at[pl.ds(0, PB), :] if source else head_raw
            return chain(src, head_raw, col_send.at[j], col_recv.at[j])
        columns = pl.ds((j - 1) * chunk, chunk)
        dst = col_raw.at[:, columns]
        src = cov.at[pl.ds(0, PB), columns] if source else dst
        return chain(src, dst, col_send.at[j], col_recv.at[j])

    def col_forward(j):
        @pl.when(r > 0)
        def _():
            col_copies(j, False)[0].wait_recv()

        chain_start(col_copies(j, False), r > 0)

    for i in range(3):
        diag_wait(i)
        diag_start(i, False, (r > 0) & (c == 0))

    for j in range(col_chunks + 1):
        chain_start(col_copies(j, True), r == 0)

    step_rows = row_count // (2 * ROW_CHUNKS)

    def row_copies(j, way, source):
        rows = pl.ds((2 * j + way) * step_rows, step_rows)
        dst = row_raw.at[rows, :]
        src = cov.at[rows, pl.ds(0, PB)] if source else dst
        to = after if way == 0 else before
        return remote(src, dst, row_send.at[j, way], row_recv.at[j, way], to, r)

    def forwards(way):
        return (place > 0) & ((place < n_col - 1) if way == 0 else (place > 1))

    def row_forward(j):
        for way in range(2):
            copy = row_copies(j, way, False)
            pl.when(place > 0)(lambda copy=copy: (copy.wait_recv(), None)[-1])
            pl.when(forwards(way))(lambda copy=copy: (copy.start(), None)[-1])

    for j in range(ROW_CHUNKS):
        for way in range(2):
            copy = row_copies(j, way, True)
            pl.when(place == 0)(lambda copy=copy: (copy.start(), None)[-1])

    owner = lax.div(r * need, width)
    offset = pl.multiple_of(lax.rem(r * need, width), 128)
    need_copies = [
        remote(
            head_raw.at[:, pl.ds(offset, need)], need_raw, need_send.at[k], need_recv, k, r
        )
        for k in range(n_col)
    ]
    own_need = pltpu.make_async_copy(
        head_raw.at[:, pl.ds(offset, need)], need_raw, local_sem.at[3]
    )

    def need_start():
        pl.when(r == 0)(lambda: (head_copy.wait(), None)[-1])
        for k in range(n_col):
            pl.when((c == owner) & (c != k))(lambda k=k: (need_copies[k].start(), None)[-1])
        pl.when(c == owner)(lambda: (own_need.start(), None)[-1])

    @pl.when(first)
    def _():
        for i in range(3):
            blocks[i] = diag[pl.ds(quarters[i][0], HALF), pl.ds(quarters[i][1], HALF)]

    unit = (
        lax.broadcasted_iota(jnp.int32, (HALF, HALF), 0)
        == lax.broadcasted_iota(jnp.int32, (HALF, HALF), 1)
    ).astype(jnp.float32)
    events = [lambda: (col_forward(0), need_start())]
    for j in range(max(col_chunks, ROW_CHUNKS)):
        if j < ROW_CHUNKS:
            events.append(lambda j=j: row_forward(j))
        if j < col_chunks:
            events.append(lambda j=j: col_forward(j + 1))

    def half(block, where):
        s_ref[...] = block
        m_ref[...] = unit
        for start in range(0, HALF, SEGMENT):
            pivots(s_ref, m_ref, r_ref, start, SEGMENT)
            if events:
                events.pop(0)()

    half(blocks[0], 0)
    inverse_11 = m_ref[...]
    inverse_ref[pl.ds(0, HALF), pl.ds(0, HALF)] = inverse_11
    inverse_ref[pl.ds(0, HALF), pl.ds(HALF, HALF)] = jnp.zeros((HALF, HALF), jnp.float32)
    factor_ref[pl.ds(0, HALF), pl.ds(0, HALF)] = r_ref[...].T
    factor_ref[pl.ds(0, HALF), pl.ds(HALF, HALF)] = jnp.zeros((HALF, HALF), jnp.float32)
    lower = dot(blocks[1], inverse_11, ((1,), (1,)))
    factor_ref[pl.ds(HALF, HALF), pl.ds(0, HALF)] = lower
    half(blocks[2] - dot(lower, lower, ((1,), (1,))), 1)
    inverse_22 = m_ref[...]
    inverse_ref[pl.ds(HALF, HALF), pl.ds(HALF, HALF)] = inverse_22
    factor_ref[pl.ds(HALF, HALF), pl.ds(HALF, HALF)] = r_ref[...].T
    lower = factor_ref[pl.ds(HALF, HALF), pl.ds(0, HALF)]
    inverse_ref[pl.ds(HALF, HALF), pl.ds(0, HALF)] = -dot(
        inverse_22, dot(lower, inverse_ref[pl.ds(0, HALF), pl.ds(0, HALF)])
    )
    while events:
        events.pop(0)()

    pl.when(c == owner)(lambda: (own_need.wait(), None)[-1])
    pl.when(c != owner)(lambda: (need_copies[0].wait_recv(), None)[-1])
    for k in range(n_col):
        pl.when((c == owner) & (c != k))(lambda k=k: (need_copies[k].wait_send(), None)[-1])
    for i in range(3):
        down, across = diag_copies(i, True)
        chain_end(down, c == 0)
        for copy in across:
            pl.when(c == 0)(lambda copy=copy: (copy.wait_send(), None)[-1])
    for j in range(col_chunks + 1):
        chain_end(col_copies(j, False), r >= 0)
    for j in range(ROW_CHUNKS):
        for way in range(2):
            copy = row_copies(j, way, False)
            pl.when((place == 0) | forwards(way))(lambda copy=copy: (copy.wait_send(), None)[-1])
    pl.when(r == 0)(lambda: (col_copy.wait(), None)[-1])
    pl.when(c == 0)(lambda: (row_copy.wait(), None)[-1])


def update_kernel(
    cov,
    row_raw,
    targets,
    noise,
    col_raw,
    head_raw,
    need_raw,
    factor,
    inverse,
    target_cov,
    updated,
    panel,
    reconstructor,
    error_cov,
    col_high,
    col_low,
    head,
    head_high,
    head_low,
):
    t = pl.program_id(0)
    r = lax.axis_index("row")
    c = lax.axis_index("col")
    rows, cols = cov.shape
    top = (r == 0) & (t < PB // rows)

    @pl.when(t == 0)
    def _():
        whole = inverse[...]
        col_high[...], col_low[...] = split(dot(whole, col_raw[...]))
        solved = dot(whole, head_raw[...])
        head[...] = solved
        head_high[...], head_low[...] = split(solved)
        other = dot(whole, need_raw[...])
        error_cov[...] = target_cov[...] - dot(other, solved, ((0,), (0,)))

    @pl.when(jnp.logical_not(top))
    def _():
        solved = dot(row_raw[...], inverse[...], ((1,), (1,)))
        panel[...] = solved
        left = split(solved)
        updated[...] = cov[...] - dot_split(left, (col_high[...], col_low[...]))
        reconstructor[...] = targets[...] - dot_split(left, (head_high[...], head_low[...]))
        start = r * (rows * pl.num_programs(0)) + t * rows - c * cols

        @pl.when((start >= 0) & (start < cols))
        def _():
            columns = pl.ds(pl.multiple_of(start, rows), rows)
            diagonal = lax.broadcasted_iota(jnp.int32, (rows, rows), 0) == (
                lax.broadcasted_iota(jnp.int32, (rows, rows), 1)
            )
            updated[:, columns] = updated[:, columns] + jnp.where(diagonal, noise[0], 0.0)

    @pl.when(top)
    def _():
        block = pl.ds(pl.multiple_of(jnp.minimum(t, PB // rows - 1) * rows, rows), rows)
        panel[...] = factor[block, :]
        updated[...] = jnp.zeros_like(updated)
        reconstructor[...] = head[block, :]

    @pl.when(c == 0)
    def _():
        updated[:, pl.ds(0, PB)] = panel[...]


def local(
    n_row, n_col, covariance, wfs_map, noise_var, targets, target_pos, layer_strength,
    layer_scale, tile_layer
):
    row_count, col_count = covariance.shape
    target_width = targets.shape[1]
    row_index = lax.axis_index("row")
    col_index = lax.axis_index("col")
    kinds = jnp.arange(noise_var.shape[0], dtype=jnp.int32)
    noise_rows = jnp.sum(
        jnp.where(wfs_map[None, :] == kinds[:, None], noise_var[:, None], 0.0), axis=0
    )
    diag = covariance[:PB, :PB] + jnp.where(
        jnp.arange(PB)[:, None] == jnp.arange(PB)[None, :], noise_rows[None, :PB], 0.0
    )
    error_rows = target_width * n_col // n_row
    col_chunks = chunks_of(col_count)
    row_start = row_index * error_rows
    col_start = col_index * target_width
    layer_all = jnp.repeat(tile_layer, TILE)
    target_cov = target_covariance(
        lax.dynamic_slice_in_dim(target_pos, row_start, error_rows, 1),
        lax.dynamic_slice_in_dim(target_pos, col_start, target_width, 1),
        lax.dynamic_slice_in_dim(layer_all, row_start, error_rows, 0),
        lax.dynamic_slice_in_dim(layer_all, col_start, target_width, 0),
        layer_strength,
        layer_scale,
    )

    def f32(*shape):
        return jax.ShapeDtypeStruct(shape, jnp.float32)

    vmem = pl.BlockSpec(memory_space=pltpu.VMEM)
    anywhere = pl.BlockSpec(memory_space=pl.ANY)
    dma = pltpu.SemaphoreType.DMA
    row_raw, col_raw, head_raw, need_raw, factor, inverse = pl.pallas_call(
        functools.partial(exchange_kernel, n_row, n_col),
        out_shape=(
            f32(row_count, PB),
            f32(PB, col_count),
            f32(PB, target_width),
            f32(PB, error_rows),
            f32(PB, PB),
            f32(PB, PB),
        ),
        in_specs=[anywhere, anywhere, vmem],
        out_specs=[vmem] * 6,
        scratch_shapes=[
            pltpu.VMEM((3, HALF, HALF), jnp.float32),
            pltpu.VMEM((HALF, HALF), jnp.float32),
            pltpu.VMEM((HALF, HALF), jnp.float32),
            pltpu.VMEM((HALF, HALF), jnp.float32),
            dma((4,)),
            dma((3, n_col + 1)),
            dma((3,)),
            dma((col_chunks + 1, 2)),
            dma((col_chunks + 1,)),
            dma((ROW_CHUNKS, 2)),
            dma((ROW_CHUNKS, 2)),
            dma((n_col,)),
            dma,
        ],
        compiler_params=pltpu.CompilerParams(
            collective_id=0, has_side_effects=True, vmem_limit_bytes=24 * 1024 * 1024
        ),
        name="exchange",
    )(covariance, targets, diag)

    def tiled(width):
        return pl.BlockSpec((ROWS, width), lambda t: (t, 0))

    def held(height, width):
        return pl.BlockSpec((height, width), lambda t: (0, 0))

    return pl.pallas_call(
        update_kernel,
        grid=(row_count // ROWS,),
        out_shape=(
            f32(row_count, col_count),
            f32(row_count, PB),
            f32(row_count, target_width),
            f32(error_rows, target_width),
        ),
        in_specs=[
            tiled(col_count),
            tiled(PB),
            tiled(target_width),
            pl.BlockSpec((1, 1, ROWS), lambda t: (t, 0, 0)),
            held(PB, col_count),
            held(PB, target_width),
            held(PB, error_rows),
            held(PB, PB),
            held(PB, PB),
            held(error_rows, target_width),
        ],
        out_specs=[
            tiled(col_count),
            tiled(PB),
            tiled(target_width),
            held(error_rows, target_width),
        ],
        scratch_shapes=[
            pltpu.VMEM((PB, col_count), jnp.bfloat16),
            pltpu.VMEM((PB, col_count), jnp.bfloat16),
            pltpu.VMEM((PB, target_width), jnp.float32),
            pltpu.VMEM((PB, target_width), jnp.bfloat16),
            pltpu.VMEM((PB, target_width), jnp.bfloat16),
        ],
        compiler_params=pltpu.CompilerParams(vmem_limit_bytes=40 * 1024 * 1024),
        name="update",
    )(
        covariance,
        row_raw,
        targets,
        noise_rows.reshape(row_count // ROWS, 1, ROWS),
        col_raw,
        head_raw,
        need_raw,
        factor,
        inverse,
        target_cov,
    )


def solution(mesh):
    placed = (P("row", "col"), P("row"), P(), P("row", "col"), P(), P(), P(), P())
    return jax.shard_map(
        functools.partial(local, mesh.shape["row"], mesh.shape["col"]),
        mesh=mesh,
        in_specs=placed,
        out_specs=(P("row", "col"), P("row", None), P("row", "col"), P("row", "col")),
        check_vma=False,
    )
```

time: 454 us -> 234 us (0.52)
  the two profiles are of different devices: /device:TPU:30 before, /device:TPU:27 now
where the time goes in v1:
time: 234 us; the launch traced here: 233 us
  Pallas kernels  214 us (91%)
  local copies, waits for them, and re-layouts  10.2 us (4%)
  other arithmetic  8.21 us (4%)
    pallas_call x1, Pallas kernels, local(): pl.pallas_call(functools.partial(exchange_kernel, n_row, n_col), out_shap...  185 us
    pallas_call x1, Pallas kernels, local(): pl.pallas_call(update_kernel, grid=(row_count // ROWS,), out_shape=(f32(r...  29.4 us
    unnamed x8, local copies, waits for them, and re-layouts  8.27 us
    reduce_sum x1, other arithmetic, target_covariance(): jnp.sum(jnp.where(levels[:, None, None] <= lowest[None], weights, 0.0), a...  5.34 us

profile of v1, /device:TPU:27, one launch (start us, length us, event | category | flops | bytes accessed | tf_op | source)
XLA Modules:
  0.0 233.2 jit_solution(5441334820402634304)
XLA Ops:
  0.6 0.0 copy-start
  0.6 0.0 copy-start.3
  0.7 0.8 mul.11
  1.5 0.9 constant_dynamic-slice_fusion
  2.4 0.8 constant_dynamic-slice_fusion.1
  3.2 0.8 select_reduce_fusion
  4.1 0.0 copy-done
  4.1 0.1 broadcast_bitcast_fusion
  4.2 0.1 dynamic_slice.12
  4.2 0.1 dynamic_slice.13
  4.3 1.0 select_add_fusion.diag
  5.3 0.2 multiply_add_fusion
  5.4 0.1 broadcast_minimum_fusion
  5.6 5.3 %fusion.2.target_cov = f32[256,512]{1,0:T(8,128)S(1)} fusion(f32[35]{0:T(128)S(1)} %mul.11, f32[256,512]{1,0:T(8,128)S(1)} %multiply_add_fusion, f32[35]{0:T(128)} %param.13, s32[256,512]{1,0:T(8,128)S(1)} %broadcast_minimum_fusion), kind=kLoop, calls=%fused_computation.4 | loop fusion | flops 27394048 | bytes 1573144 | tf_op jit(solution)/shard_map/reduce_sum | solution.py:52
  10.9 0.0 copy-start.1
  10.9 6.4 %copy-done.1 = f32[1536,3072]{1,0:T(8,128)S(1)} copy-done((f32[1536,3072]{1,0:T(8,128)S(1)}, f32[1536,3072]{1,0:T(8,128)}, u32[]{:S(2)}) %copy-start.1) | copy-done | bytes 18874392
  17.3 0.0 copy-start.2
  17.3 1.9 copy-done.2
  19.2 184.6 %exchange.1 = (f32[1536,256]{1,0:T(8,128)S(1)}, f32[256,3072]{1,0:T(8,128)S(1)}, f32[256,512]{1,0:T(8,128)S(1)}, f32[256,256]{1,0:T(8,128)S(1)}, f32[256,256]{1,0:T(8,128)S(1)}, /*index=5*/f32[256,256]{1,0:T(8,128)S(1)}) custom-call(f32[1536,3072]{1,0:T(8,128)S(1)} %copy-done.1, f32[1536,512]{1,0:T(8,128)S(1)} %copy-done.2, f32[256,256]{1,0:T(8,128)S(1)} %select_add_fusion.diag), custom_call_target="tpu_custom_call" | custom-call | tf_op jit(solution)/shard_map/exchange/pallas_call | solution.py:431
  203.8 0.0 copy-done.3
  203.8 29.4 %update.1 = (f32[1536,3072]{1,0:T(8,128)}, f32[1536,256]{1,0:T(8,128)}, f32[1536,512]{1,0:T(8,128)}, f32[256,512]{1,0:T(8,128)}) custom-call(f32[1536,3072]{1,0:T(8,128)} %cov.3, f32[1536,256]{1,0:T(8,128)S(1)} %get-tuple-element.10.row_raw, f32[1536,512]{1,0:T(8,128)S(1)} %copy-done.3, f32[12,1,128]{2,1,0:T(1,128)S(1)} %reshape.109.noise, ...), custom_call_target="tpu_custom_call" | custom-call | tf_op jit(solution)/shard_map/update/pallas_call | solution.py:470
  (2 shorter events, 0.0 us)
Async XLA Ops:
  0.6 3.4 %copy-start = (s32[16]{0:T(128)S(1)}, s32[16]{0:T(128)}, u32[]{:S(2)}) copy-start(s32[16]{0:T(128)} %param.15) | copy-start | bytes 196
  0.6 203.2 %copy-start.3 = (f32[1536,512]{1,0:T(8,128)S(1)}, f32[1536,512]{1,0:T(8,128)}, u32[]{:S(2)}) copy-start(f32[1536,512]{1,0:T(8,128)} %targets.3) | copy-start | bytes 9437188
  10.9 6.4 %copy-start.1 = (f32[1536,3072]{1,0:T(8,128)S(1)}, f32[1536,3072]{1,0:T(8,128)}, u32[]{:S(2)}) copy-start(f32[1536,3072]{1,0:T(8,128)} %cov.3) | copy-start | bytes 56623108
  17.3 1.9 copy-start.2

commit v2 on v1

--- a/solution.py
+++ b/solution.py
@@ -10,7 +10,6 @@
 PB = 256
 TILE = 128
 HALF = PB // 2
-ROWS = 128
 CHUNKS = 8
 ROW_CHUNKS = 6
 SEGMENT = 16
@@ -40,16 +39,32 @@
     return total + jnp.dot(a[0], b[1], preferred_element_type=jnp.float32)
 
 
-def target_covariance(pos_rows, pos_cols, layer_rows, layer_cols, layer_strength, layer_scale):
-    distance = (pos_rows[0][:, None] - pos_cols[0][None, :]) ** 2 + (
-        pos_rows[1][:, None] - pos_cols[1][None, :]
-    ) ** 2
-    lowest = jnp.minimum(layer_rows[:, None], layer_cols[None, :])
-    levels = jnp.arange(layer_strength.shape[0], dtype=jnp.int32)
-    weights = layer_strength[:, None, None] / (
-        1.0 + distance[None] / (layer_scale * layer_scale)[:, None, None]
-    )
-    return jnp.sum(jnp.where(levels[:, None, None] <= lowest[None], weights, 0.0), axis=0)
+def target_covariance(out, pos, strength, inverse_square, tile_layer, row_start, col_start):
+    height, width = out.shape
+    levels = strength.shape[0]
+
+    def upright(axis):
+        line = pos[pl.ds(axis, 1), pl.ds(row_start, height)]
+        return jnp.broadcast_to(line, (TILE, height)).T
+
+    rows = [upright(0), upright(1)]
+    for i in range(height // TILE):
+        for j in range(width // TILE):
+            columns = pl.ds(pl.multiple_of(col_start + j * TILE, TILE), TILE)
+            across = rows[0][i * TILE : (i + 1) * TILE] - pos[pl.ds(0, 1), columns]
+            along = rows[1][i * TILE : (i + 1) * TILE] - pos[pl.ds(1, 1), columns]
+            distance = across * across + along * along
+            lowest = jnp.minimum(
+                tile_layer[row_start // TILE + i], tile_layer[col_start // TILE + j]
+            )
+
+            def layer(l, total, distance=distance, lowest=lowest):
+                weight = jnp.where(l <= lowest, strength[l], 0.0)
+                return total + weight / (1.0 + distance * inverse_square[l])
+
+            out[pl.ds(i * TILE, TILE), pl.ds(j * TILE, TILE)] = lax.fori_loop(
+                0, levels, layer, jnp.zeros_like(distance)
+            )
 
 
 def gray_neighbours(c, n):
@@ -64,27 +79,37 @@
     return position, after, before
 
 
-def pivots(s_ref, m_ref, r_ref, start, count):
-    n = s_ref.shape[0]
-    lanes = lax.broadcasted_iota(jnp.int32, (n, n), 1)
-    lane = lax.broadcasted_iota(jnp.int32, (1, n), 1)
-    down = lax.broadcasted_iota(jnp.int32, (n, 1), 0)
-
-    def step(k, carry):
-        row = s_ref[pl.ds(k, 1), :]
-        inverse_row = m_ref[pl.ds(k, 1), :]
-        whole = s_ref[...]
-        column = jnp.sum(jnp.where(lanes == k, whole, 0.0), axis=1, keepdims=True)
-        pivot = jnp.sum(jnp.where(lane == k, row, 0.0), axis=1, keepdims=True)
-        root = lax.rsqrt(pivot)
-        factor = jnp.where(down > k, column * (1.0 / pivot), 0.0)
-        r_ref[pl.ds(k, 1), :] = jnp.where(lane >= k, row * root, 0.0)
-        s_ref[...] = whole - factor * row
-        scaled = m_ref[...] - factor * inverse_row
-        m_ref[...] = jnp.where(down == k, scaled * root, scaled)
+def pivots(t_ref, start, count):
+    n = t_ref.shape[0]
+    lanes = lax.broadcasted_iota(jnp.int32, (8, n), 1)
+    wide = lax.broadcasted_iota(jnp.int32, (8, 2 * n), 1)
+    down = lax.broadcasted_iota(jnp.int32, (8, 1), 0)
+
+    def step(i, carry):
+        k = pl.multiple_of(i * 8, 8)
+        rows = t_ref[pl.ds(k, 8), :]
+        left = rows[:, :n]
+        columns = [
+            jnp.sum(jnp.where(lanes == k + j, left, 0.0), axis=1, keepdims=True)
+            for j in range(8)
+        ]
+        scale = jnp.ones((8, 1), jnp.float32)
+        for j in range(8):
+            pivot = columns[j][j : j + 1]
+            scale = jnp.where(down == j, lax.rsqrt(pivot), scale)
+            if j < 7:
+                factor = jnp.where(down > j, columns[j] * (1.0 / pivot), 0.0)
+                rows = rows - factor * rows[j : j + 1]
+                for later in range(j + 1, 8):
+                    columns[later] = columns[later] - factor * columns[later][j : j + 1]
+        rows = rows * scale
+        rows = jnp.where((wide >= n) | (wide >= k + down), rows, 0.0)
+        below = jnp.where(lanes >= k + 8, rows[:, :n], 0.0)
+        t_ref[...] = t_ref[...] - dot(below, rows, ((0,), (0,)))
+        t_ref[pl.ds(k, 8), :] = rows
         return carry
 
-    lax.fori_loop(start, start + count, step, 0)
+    lax.fori_loop(start // 8, (start + count) // 8, step, 0)
 
 
 def exchange_kernel(
@@ -93,16 +118,19 @@
     cov,
     targets,
     diag,
+    pos,
+    strength,
+    inverse_square,
+    tile_layer,
     row_raw,
     col_raw,
     head_raw,
     need_raw,
     factor_ref,
     inverse_ref,
+    target_cov,
     blocks,
-    s_ref,
-    m_ref,
-    r_ref,
+    t_ref,
     local_sem,
     diag_send,
     diag_recv,
@@ -211,11 +239,21 @@
         return chain(src, dst, col_send.at[j], col_recv.at[j])
 
     def col_forward(j):
-        @pl.when(r > 0)
+        @pl.when((r > 0) & even)
         def _():
             col_copies(j, False)[0].wait_recv()
 
         chain_start(col_copies(j, False), r > 0)
+
+    target_covariance(
+        target_cov,
+        pos,
+        strength,
+        inverse_square,
+        tile_layer,
+        pl.multiple_of(r * need, 128),
+        pl.multiple_of(c * width, 128),
+    )
 
     for i in range(3):
         diag_wait(i)
@@ -239,8 +277,7 @@
     def row_forward(j):
         for way in range(2):
             copy = row_copies(j, way, False)
-            pl.when(place > 0)(lambda copy=copy: (copy.wait_recv(), None)[-1])
-            pl.when(forwards(way))(lambda copy=copy: (copy.start(), None)[-1])
+            pl.when(forwards(way))(lambda copy=copy: (copy.wait_recv(), copy.start(), None)[-1])
 
     for j in range(ROW_CHUNKS):
         for way in range(2):
@@ -261,6 +298,9 @@
 
     def need_start():
         pl.when(r == 0)(lambda: (head_copy.wait(), None)[-1])
+        pl.when((r > 0) & ~even & (c == owner))(
+            lambda: (col_copies(0, False)[0].wait_recv(), None)[-1]
+        )
         for k in range(n_col):
             pl.when((c == owner) & (c != k))(lambda k=k: (need_copies[k].start(), None)[-1])
         pl.when(c == owner)(lambda: (own_need.start(), None)[-1])
@@ -274,33 +314,33 @@
         lax.broadcasted_iota(jnp.int32, (HALF, HALF), 0)
         == lax.broadcasted_iota(jnp.int32, (HALF, HALF), 1)
     ).astype(jnp.float32)
-    events = [lambda: (col_forward(0), need_start())]
+    events = [lambda: row_forward(0), lambda: (col_forward(0), need_start(), row_forward(1))]
     for j in range(max(col_chunks, ROW_CHUNKS)):
-        if j < ROW_CHUNKS:
-            events.append(lambda j=j: row_forward(j))
+        if j + 2 < ROW_CHUNKS:
+            events.append(lambda j=j: row_forward(j + 2))
         if j < col_chunks:
             events.append(lambda j=j: col_forward(j + 1))
 
     def half(block, where):
-        s_ref[...] = block
-        m_ref[...] = unit
+        t_ref[:, pl.ds(0, HALF)] = block
+        t_ref[:, pl.ds(HALF, HALF)] = unit
         for start in range(0, HALF, SEGMENT):
-            pivots(s_ref, m_ref, r_ref, start, SEGMENT)
+            pivots(t_ref, start, SEGMENT)
             if events:
                 events.pop(0)()
 
     half(blocks[0], 0)
-    inverse_11 = m_ref[...]
+    inverse_11 = t_ref[:, pl.ds(HALF, HALF)]
     inverse_ref[pl.ds(0, HALF), pl.ds(0, HALF)] = inverse_11
     inverse_ref[pl.ds(0, HALF), pl.ds(HALF, HALF)] = jnp.zeros((HALF, HALF), jnp.float32)
-    factor_ref[pl.ds(0, HALF), pl.ds(0, HALF)] = r_ref[...].T
+    factor_ref[pl.ds(0, HALF), pl.ds(0, HALF)] = t_ref[:, pl.ds(0, HALF)].T
     factor_ref[pl.ds(0, HALF), pl.ds(HALF, HALF)] = jnp.zeros((HALF, HALF), jnp.float32)
     lower = dot(blocks[1], inverse_11, ((1,), (1,)))
     factor_ref[pl.ds(HALF, HALF), pl.ds(0, HALF)] = lower
     half(blocks[2] - dot(lower, lower, ((1,), (1,))), 1)
-    inverse_22 = m_ref[...]
+    inverse_22 = t_ref[:, pl.ds(HALF, HALF)]
     inverse_ref[pl.ds(HALF, HALF), pl.ds(HALF, HALF)] = inverse_22
-    factor_ref[pl.ds(HALF, HALF), pl.ds(HALF, HALF)] = r_ref[...].T
+    factor_ref[pl.ds(HALF, HALF), pl.ds(HALF, HALF)] = t_ref[:, pl.ds(0, HALF)].T
     lower = factor_ref[pl.ds(HALF, HALF), pl.ds(0, HALF)]
     inverse_ref[pl.ds(HALF, HALF), pl.ds(0, HALF)] = -dot(
         inverse_22, dot(lower, inverse_ref[pl.ds(0, HALF), pl.ds(0, HALF)])
@@ -308,6 +348,13 @@
     while events:
         events.pop(0)()
 
+    for j in range(col_chunks + 1):
+        late = ~even & (c != owner) if j == 0 else ~even
+        pl.when(late)(lambda j=j: (col_copies(j, False)[0].wait_recv(), None)[-1])
+    for j in range(ROW_CHUNKS):
+        for way in range(2):
+            copy = row_copies(j, way, False)
+            pl.when((place > 0) & ~forwards(way))(lambda copy=copy: (copy.wait_recv(), None)[-1])
     pl.when(c == owner)(lambda: (own_need.wait(), None)[-1])
     pl.when(c != owner)(lambda: (need_copies[0].wait_recv(), None)[-1])
     for k in range(n_col):
@@ -342,8 +389,9 @@
     panel,
     reconstructor,
     error_cov,
-    col_high,
-    col_low,
+    left,
+    left_high,
+    left_low,
     head,
     head_high,
     head_low,
@@ -352,45 +400,55 @@
     r = lax.axis_index("row")
     c = lax.axis_index("col")
     rows, cols = cov.shape
-    top = (r == 0) & (t < PB // rows)
+    part = panel.shape[0]
 
     @pl.when(t == 0)
     def _():
         whole = inverse[...]
-        col_high[...], col_low[...] = split(dot(whole, col_raw[...]))
+        solved = dot(row_raw[...], whole, ((1,), (1,)))
+        left[...] = solved
+        left_high[...], left_low[...] = split(solved)
+
+        @pl.when(r == 0)
+        def _():
+            left[pl.ds(0, PB), :] = factor[...]
+
         solved = dot(whole, head_raw[...])
         head[...] = solved
         head_high[...], head_low[...] = split(solved)
         other = dot(whole, need_raw[...])
         error_cov[...] = target_cov[...] - dot(other, solved, ((0,), (0,)))
 
-    @pl.when(jnp.logical_not(top))
+    here = pl.ds(pl.multiple_of(t * part, part), part)
+    panel[...] = left[here, :]
+    reconstructor[...] = targets[...] - dot_split(
+        (left_high[here, :], left_low[here, :]), (head_high[...], head_low[...])
+    )
+
+    @pl.when((r == 0) & (t < PB // part))
     def _():
-        solved = dot(row_raw[...], inverse[...], ((1,), (1,)))
-        panel[...] = solved
-        left = split(solved)
-        updated[...] = cov[...] - dot_split(left, (col_high[...], col_low[...]))
-        reconstructor[...] = targets[...] - dot_split(left, (head_high[...], head_low[...]))
-        start = r * (rows * pl.num_programs(0)) + t * rows - c * cols
-
-        @pl.when((start >= 0) & (start < cols))
-        def _():
-            columns = pl.ds(pl.multiple_of(start, rows), rows)
-            diagonal = lax.broadcasted_iota(jnp.int32, (rows, rows), 0) == (
-                lax.broadcasted_iota(jnp.int32, (rows, rows), 1)
-            )
-            updated[:, columns] = updated[:, columns] + jnp.where(diagonal, noise[0], 0.0)
-
-    @pl.when(top)
+        block = pl.ds(pl.multiple_of(jnp.minimum(t, PB // part - 1) * part, part), part)
+        reconstructor[...] = head[block, :]
+
+    right = split(dot(inverse[...], col_raw[...]))
+    updated[...] = cov[...] - dot_split((left_high[...], left_low[...]), right)
+    start = c * (cols * pl.num_programs(0)) + t * cols - r * rows
+
+    @pl.when((start >= 0) & (start < rows))
     def _():
-        block = pl.ds(pl.multiple_of(jnp.minimum(t, PB // rows - 1) * rows, rows), rows)
-        panel[...] = factor[block, :]
-        updated[...] = jnp.zeros_like(updated)
-        reconstructor[...] = head[block, :]
-
-    @pl.when(c == 0)
+        block = pl.ds(pl.multiple_of(start, cols), cols)
+        diagonal = lax.broadcasted_iota(jnp.int32, (cols, cols), 0) == (
+            lax.broadcasted_iota(jnp.int32, (cols, cols), 1)
+        )
+        updated[block, :] = updated[block, :] + jnp.where(diagonal, noise[start // cols], 0.0)
+
+    @pl.when(r == 0)
     def _():
-        updated[:, pl.ds(0, PB)] = panel[...]
+        updated[pl.ds(0, PB), :] = jnp.zeros((PB, cols), jnp.float32)
+
+    @pl.when((c == 0) & (t == 0))
+    def _():
+        updated[...] = left[...]
 
 
 def local(
@@ -399,8 +457,6 @@
 ):
     row_count, col_count = covariance.shape
     target_width = targets.shape[1]
-    row_index = lax.axis_index("row")
-    col_index = lax.axis_index("col")
     kinds = jnp.arange(noise_var.shape[0], dtype=jnp.int32)
     noise_rows = jnp.sum(
         jnp.where(wfs_map[None, :] == kinds[:, None], noise_var[:, None], 0.0), axis=0
@@ -410,25 +466,14 @@
     )
     error_rows = target_width * n_col // n_row
     col_chunks = chunks_of(col_count)
-    row_start = row_index * error_rows
-    col_start = col_index * target_width
-    layer_all = jnp.repeat(tile_layer, TILE)
-    target_cov = target_covariance(
-        lax.dynamic_slice_in_dim(target_pos, row_start, error_rows, 1),
-        lax.dynamic_slice_in_dim(target_pos, col_start, target_width, 1),
-        lax.dynamic_slice_in_dim(layer_all, row_start, error_rows, 0),
-        lax.dynamic_slice_in_dim(layer_all, col_start, target_width, 0),
-        layer_strength,
-        layer_scale,
-    )
-
     def f32(*shape):
         return jax.ShapeDtypeStruct(shape, jnp.float32)
 
     vmem = pl.BlockSpec(memory_space=pltpu.VMEM)
-    anywhere = pl.BlockSpec(memory_space=pl.ANY)
+    anywhere = pl.BlockSpec(memory_space=pltpu.HBM)
+    smem = pl.BlockSpec(memory_space=pltpu.SMEM)
     dma = pltpu.SemaphoreType.DMA
-    row_raw, col_raw, head_raw, need_raw, factor, inverse = pl.pallas_call(
+    row_raw, col_raw, head_raw, need_raw, factor, inverse, target_cov = pl.pallas_call(
         functools.partial(exchange_kernel, n_row, n_col),
         out_shape=(
             f32(row_count, PB),
@@ -437,14 +482,13 @@
             f32(PB, error_rows),
             f32(PB, PB),
             f32(PB, PB),
+            f32(error_rows, target_width),
         ),
-        in_specs=[anywhere, anywhere, vmem],
-        out_specs=[vmem] * 6,
+        in_specs=[anywhere, anywhere, vmem, vmem, smem, smem, smem],
+        out_specs=[vmem] * 7,
         scratch_shapes=[
             pltpu.VMEM((3, HALF, HALF), jnp.float32),
-            pltpu.VMEM((HALF, HALF), jnp.float32),
-            pltpu.VMEM((HALF, HALF), jnp.float32),
-            pltpu.VMEM((HALF, HALF), jnp.float32),
+            pltpu.VMEM((HALF, PB), jnp.float32),
             dma((4,)),
             dma((3, n_col + 1)),
             dma((3,)),
@@ -456,20 +500,34 @@
             dma,
         ],
         compiler_params=pltpu.CompilerParams(
-            collective_id=0, has_side_effects=True, vmem_limit_bytes=24 * 1024 * 1024
+            collective_id=0, has_side_effects=True, vmem_limit_bytes=52 * 1024 * 1024
         ),
         name="exchange",
-    )(covariance, targets, diag)
+    )(
+        covariance,
+        targets,
+        diag,
+        target_pos,
+        layer_strength,
+        1.0 / (layer_scale * layer_scale),
+        tile_layer,
+    )
+
+    steps = col_count // PB
+    part = row_count // steps
 
     def tiled(width):
-        return pl.BlockSpec((ROWS, width), lambda t: (t, 0))
+        return pl.BlockSpec((part, width), lambda t: (t, 0))
+
+    def across(height):
+        return pl.BlockSpec((height, PB), lambda t: (0, t))
 
     def held(height, width):
         return pl.BlockSpec((height, width), lambda t: (0, 0))
 
     return pl.pallas_call(
         update_kernel,
-        grid=(row_count // ROWS,),
+        grid=(steps,),
         out_shape=(
             f32(row_count, col_count),
             f32(row_count, PB),
@@ -477,11 +535,11 @@
             f32(error_rows, target_width),
         ),
         in_specs=[
-            tiled(col_count),
-            tiled(PB),
+            across(row_count),
+            held(row_count, PB),
             tiled(target_width),
-            pl.BlockSpec((1, 1, ROWS), lambda t: (t, 0, 0)),
-            held(PB, col_count),
+            pl.BlockSpec((row_count // PB, 1, PB), lambda t: (0, 0, 0)),
+            across(PB),
             held(PB, target_width),
             held(PB, error_rows),
             held(PB, PB),
@@ -489,14 +547,15 @@
             held(error_rows, target_width),
         ],
         out_specs=[
-            tiled(col_count),
+            across(row_count),
             tiled(PB),
             tiled(target_width),
             held(error_rows, target_width),
         ],
         scratch_shapes=[
-            pltpu.VMEM((PB, col_count), jnp.bfloat16),
-            pltpu.VMEM((PB, col_count), jnp.bfloat16),
+            pltpu.VMEM((row_count, PB), jnp.float32),
+            pltpu.VMEM((row_count, PB), jnp.bfloat16),
+            pltpu.VMEM((row_count, PB), jnp.bfloat16),
             pltpu.VMEM((PB, target_width), jnp.float32),
             pltpu.VMEM((PB, target_width), jnp.bfloat16),
             pltpu.VMEM((PB, target_width), jnp.bfloat16),
@@ -507,7 +566,7 @@
         covariance,
         row_raw,
         targets,
-        noise_rows.reshape(row_count // ROWS, 1, ROWS),
+        noise_rows.reshape(row_count // PB, 1, PB),
         col_raw,
         head_raw,
         need_raw,

time: 234 us -> 128 us (0.55)
  the two profiles are of different devices: /device:TPU:27 before, /device:TPU:30 now
where the time goes in v2:
time: 128 us; the launch traced here: 127 us
  Pallas kernels  118 us (92%)
  local copies, waits for them, and re-layouts  6.37 us (5%)
  other arithmetic  2.44 us (2%)
    pallas_call x1, Pallas kernels, local(): pl.pallas_call(functools.partial(exchange_kernel, n_row, n_col), out_shap...  86.6 us
    pallas_call x1, Pallas kernels, local(): pl.pallas_call(update_kernel, grid=(steps,), out_shape=(f32(row_count, co...  31.3 us
    unnamed x14, local copies, waits for them, and re-layouts  6.36 us

profile of v2, /device:TPU:30, one launch (start us, length us, event | category | flops | bytes accessed | tf_op | source)
XLA Modules:
  0.0 127.4 jit_solution(7233646270053750618)
XLA Ops:
  0.6 0.7 multiply_divide_fusion.inverse_square
  1.3 0.8 select_reduce_fusion
  2.1 1.0 select_add_fusion.diag
  3.1 0.0 copy-start.4
  3.1 0.7 copy-done.4
  3.8 0.0 copy-start.5
  3.8 0.7 copy-done.5
  4.5 0.0 copy-start.6
  4.5 0.7 copy-done.6
  5.1 0.0 copy-start
  5.1 86.6 %exchange.1 = (f32[1536,256]{1,0:T(8,128)}, f32[256,3072]{1,0:T(8,128)}, f32[256,512]{1,0:T(8,128)S(1)}, f32[256,256]{1,0:T(8,128)S(1)}, f32[256,256]{1,0:T(8,12...) custom-call(f32[1536,3072]{1,0:T(8,128)} %cov.3, f32[1536,512]{1,0:T(8,128)} %targets.3, ...), custom_call_target="tpu_custom_call" | custom-call | tf_op jit(solution)/shard_map/exchange/pallas_call | solution.py:476
  91.8 0.0 copy-done
  91.8 0.0 copy-start.1
  91.8 1.9 %copy-done.1 = f32[256,3072]{1,0:T(8,128)S(1)} copy-done((f32[256,3072]{1,0:T(8,128)S(1)}, f32[256,3072]{1,0:T(8,128)}, u32[]{:S(2)}) %copy-start.1) | copy-done | bytes 3145752
  93.7 0.0 copy-start.2
  93.7 1.4 %copy-done.2 = f32[1536,256]{1,0:T(8,128)S(1)} copy-done((f32[1536,256]{1,0:T(8,128)S(1)}, f32[1536,256]{1,0:T(8,128)}, u32[]{:S(2)}) %copy-start.2) | copy-done | bytes 1572888
  95.1 0.0 copy-start.3
  95.1 1.0 copy-done.3
  96.1 31.3 %update.1 = (f32[1536,3072]{1,0:T(8,128)}, f32[1536,256]{1,0:T(8,128)}, f32[1536,512]{1,0:T(8,128)}, f32[256,512]{1,0:T(8,128)}) custom-call(f32[1536,3072]{1,0:T(8,128)} %cov.3, f32[1536,256]{1,0:T(8,128)S(1)} %copy-done.2, f32[1536,512]{1,0:T(8,128)S(1)} %copy-done, f32[6,1,256]{2,1,0:T(1,128)S(1)} %reshape.14.noise, f32[256,3072]{1,0:T(8,128)S(1)} %copy-done.1, ...), custom_call_target="tpu_custom_call" | custom-call | tf_op jit(solution)/shard_map/update/pallas_call | solution.py:528
  (2 shorter events, 0.0 us)
Async XLA Ops:
  3.1 0.7 copy-start.4
  3.8 0.7 copy-start.5
  4.5 0.7 copy-start.6
  5.1 86.6 %copy-start = (f32[1536,512]{1,0:T(8,128)S(1)}, f32[1536,512]{1,0:T(8,128)}, u32[]{:S(2)}) copy-start(f32[1536,512]{1,0:T(8,128)} %targets.3) | copy-start | bytes 9437188
  91.8 1.9 %copy-start.1 = (f32[256,3072]{1,0:T(8,128)S(1)}, f32[256,3072]{1,0:T(8,128)}, u32[]{:S(2)}) copy-start(f32[256,3072]{1,0:T(8,128)} %get-tuple-element.12.col_raw) | copy-start | bytes 9437188
  93.7 1.4 %copy-start.2 = (f32[1536,256]{1,0:T(8,128)S(1)}, f32[1536,256]{1,0:T(8,128)}, u32[]{:S(2)}) copy-start(f32[1536,256]{1,0:T(8,128)} %get-tuple-element.11.row_raw) | copy-start | bytes 4718596
  95.1 1.0 copy-start.3

commit v3 on v2

--- a/solution.py
+++ b/solution.py
@@ -24,6 +24,23 @@
     )
 
 
+def outer(a, b):
+    def thirds(x):
+        high = x.astype(jnp.bfloat16).astype(jnp.float32)
+        middle = (x - high).astype(jnp.bfloat16).astype(jnp.float32)
+        return high, middle, x - high - middle
+
+    p, q = thirds(a), thirds(b)
+    left = jnp.concatenate([p[0], p[0], p[1], p[0], p[2], p[1]], axis=0)
+    right = jnp.concatenate([q[0], q[1], q[0], q[2], q[0], q[1]], axis=0)
+    return lax.dot_general(
+        left.astype(jnp.bfloat16),
+        right.astype(jnp.bfloat16),
+        (((0,), (0,)), ((), ())),
+        preferred_element_type=jnp.float32,
+    )
+
+
 def chunks_of(count):
     return max(n for n in range(1, CHUNKS + 1) if count // 128 % n == 0)
 
@@ -31,12 +48,6 @@
 def split(x):
     high = x.astype(jnp.bfloat16)
     return high, (x - high.astype(jnp.float32)).astype(jnp.bfloat16)
-
-
-def dot_split(a, b):
-    total = jnp.dot(a[0], b[0], preferred_element_type=jnp.float32)
-    total += jnp.dot(a[1], b[0], preferred_element_type=jnp.float32)
-    return total + jnp.dot(a[0], b[1], preferred_element_type=jnp.float32)
 
 
 def target_covariance(out, pos, strength, inverse_square, tile_layer, row_start, col_start):
@@ -105,7 +116,7 @@
         rows = rows * scale
         rows = jnp.where((wide >= n) | (wide >= k + down), rows, 0.0)
         below = jnp.where(lanes >= k + 8, rows[:, :n], 0.0)
-        t_ref[...] = t_ref[...] - dot(below, rows, ((0,), (0,)))
+        t_ref[...] = t_ref[...] - outer(below, rows)
         t_ref[pl.ds(k, 8), :] = rows
         return carry
 
@@ -390,11 +401,9 @@
     reconstructor,
     error_cov,
     left,
-    left_high,
-    left_low,
+    left_parts,
     head,
-    head_high,
-    head_low,
+    head_parts,
 ):
     t = pl.program_id(0)
     r = lax.axis_index("row")
@@ -407,7 +416,10 @@
         whole = inverse[...]
         solved = dot(row_raw[...], whole, ((1,), (1,)))
         left[...] = solved
-        left_high[...], left_low[...] = split(solved)
+        high, low = split(solved)
+        left_parts[:, pl.ds(0, PB)] = high
+        left_parts[:, pl.ds(PB, PB)] = low
+        left_parts[:, pl.ds(2 * PB, PB)] = high
 
         @pl.when(r == 0)
         def _():
@@ -415,14 +427,15 @@
 
         solved = dot(whole, head_raw[...])
         head[...] = solved
-        head_high[...], head_low[...] = split(solved)
+        high, low = split(solved)
+        head_parts[...] = jnp.concatenate([high, high, low], axis=0)
         other = dot(whole, need_raw[...])
         error_cov[...] = target_cov[...] - dot(other, solved, ((0,), (0,)))
 
     here = pl.ds(pl.multiple_of(t * part, part), part)
     panel[...] = left[here, :]
-    reconstructor[...] = targets[...] - dot_split(
-        (left_high[here, :], left_low[here, :]), (head_high[...], head_low[...])
+    reconstructor[...] = targets[...] - jnp.dot(
+        left_parts[here, :], head_parts[...], preferred_element_type=jnp.float32
     )
 
     @pl.when((r == 0) & (t < PB // part))
@@ -430,8 +443,12 @@
         block = pl.ds(pl.multiple_of(jnp.minimum(t, PB // part - 1) * part, part), part)
         reconstructor[...] = head[block, :]
 
-    right = split(dot(inverse[...], col_raw[...]))
-    updated[...] = cov[...] - dot_split((left_high[...], left_low[...]), right)
+    high, low = split(dot(inverse[...], col_raw[...]))
+    updated[...] = cov[...] - jnp.dot(
+        left_parts[...],
+        jnp.concatenate([high, high, low], axis=0),
+        preferred_element_type=jnp.float32,
+    )
     start = c * (cols * pl.num_programs(0)) + t * cols - r * rows
 
     @pl.when((start >= 0) & (start < rows))
@@ -500,7 +517,7 @@
             dma,
         ],
         compiler_params=pltpu.CompilerParams(
-            collective_id=0, has_side_effects=True, vmem_limit_bytes=52 * 1024 * 1024
+            collective_id=0, has_side_effects=True, vmem_limit_bytes=46 * 1024 * 1024
         ),
         name="exchange",
     )(
@@ -554,11 +571,9 @@
         ],
         scratch_shapes=[
             pltpu.VMEM((row_count, PB), jnp.float32),
-            pltpu.VMEM((row_count, PB), jnp.bfloat16),
-            pltpu.VMEM((row_count, PB), jnp.bfloat16),
+            pltpu.VMEM((row_count, 3 * PB), jnp.bfloat16),
             pltpu.VMEM((PB, target_width), jnp.float32),
-            pltpu.VMEM((PB, target_width), jnp.bfloat16),
-            pltpu.VMEM((PB, target_width), jnp.bfloat16),
+            pltpu.VMEM((3 * PB, target_width), jnp.bfloat16),
         ],
         compiler_params=pltpu.CompilerParams(vmem_limit_bytes=40 * 1024 * 1024),
         name="update",

time: 128 us -> 121 us (0.945)
  local copies, waits for them, and re-layouts: 6.37 us -> 2.04 us
  Pallas kernels: 118 us -> 115 us
    unnamed x14 -> x8, local copies, waits for them, and re-layouts: 6.36 us -> 2.03 us
    pallas_call x1, Pallas kernels: 86.6 us -> 83.4 us  [local(): pl.pallas_call(functools.partial(exchange_kernel, n_row, n_col), out_shap...]
where the time goes in v3:
time: 121 us; the launch traced here: 120 us
  Pallas kernels  115 us (95%)
  other arithmetic  2.44 us (2%)
  local copies, waits for them, and re-layouts  2.04 us (2%)
    pallas_call x1, Pallas kernels, local(): pl.pallas_call(functools.partial(exchange_kernel, n_row, n_col), out_shap...  83.4 us
    pallas_call x1, Pallas kernels, local(): pl.pallas_call(update_kernel, grid=(steps,), out_shape=(f32(row_count, co...  31.3 us

profile of v3, /device:TPU:30, one launch (start us, length us, event | category | flops | bytes accessed | tf_op | source)
XLA Modules:
  0.0 119.8 jit_solution(11428148852253734647)
XLA Ops:
  0.6 0.7 multiply_divide_fusion.inverse_square
  1.3 0.8 select_reduce_fusion
  2.1 1.0 select_add_fusion.diag
  3.1 0.0 copy-start.1
  3.1 0.7 copy-done.1
  3.8 0.0 copy-start.2
  3.8 0.7 copy-done.2
  4.5 0.0 copy-start.3
  4.5 0.7 copy-done.3
  5.1 0.0 copy-start
  5.1 83.4 %exchange.1 = (f32[1536,256]{1,0:T(8,128)S(1)}, f32[256,3072]{1,0:T(8,128)S(1)}, f32[256,512]{1,0:T(8,128)S(1)}, f32[256,256]{1,0:T(8,128)S(1)}, f32[256,256]{1,...) custom-call(f32[1536,3072]{1,0:T(8,128)} %cov.3, f32[1536,512]{1,0:T(8,128)} %targets.3, ...), custom_call_target="tpu_custom_call" | custom-call | tf_op jit(solution)/shard_map/exchange/pallas_call | solution.py:493
  88.5 0.0 copy-done
  88.6 31.3 %update.1 = (f32[1536,3072]{1,0:T(8,128)}, f32[1536,256]{1,0:T(8,128)}, f32[1536,512]{1,0:T(8,128)}, f32[256,512]{1,0:T(8,128)}) custom-call(f32[1536,3072]{1,0:T(8,128)} %cov.3, f32[1536,256]{1,0:T(8,128)S(1)} %get-tuple-element.11.row_raw, f32[1536,512]{1,0:T(8,128)S(1)} %copy-done, f32[6,1,256]{2,1,0:T(1,128)S(1)} %reshape.14.noise, ...), custom_call_target="tpu_custom_call" | custom-call | tf_op jit(solution)/shard_map/update/pallas_call | solution.py:545
  (2 shorter events, 0.0 us)
Async XLA Ops:
  3.1 0.7 copy-start.1
  3.8 0.7 copy-start.2
  4.5 0.7 copy-start.3
  5.1 83.4 %copy-start = (f32[1536,512]{1,0:T(8,128)S(1)}, f32[1536,512]{1,0:T(8,128)}, u32[]{:S(2)}) copy-start(f32[1536,512]{1,0:T(8,128)} %targets.3) | copy-start | bytes 9437188
